TPU v7x, 128 devices: a whole 4x4x4 slice. The times are simulated.
128 devices in a mesh: ctx: 32 (over x_hi, z, y), tp: 4 (over x_lo, core).
Axes of the slice: x: 4 (x_hi: 2, x_lo: 2; x = x_hi * 2 + x_lo), y: 4, z: 4, core: 2. Of those that a mesh axis runs over, the one named last changes fastest.
Arguments:
- tokens: bfloat16 [16384, 6144], P(('ctx', 'tp')), may hold values from -18 to 18
- w_query: bfloat16 [6144, 3072], P(None, 'tp'), may hold values from -1 to 1
- key_matrix: bfloat16 [6144, 512], P(None, 'tp'), may hold values from -1 to 1
- value_matrix: bfloat16 [6144, 512], P(None, 'tp'), may hold values from -0.078125 to 0.078125
- w_out: bfloat16 [3072, 6144], P('tp'), may hold values from -0.109375 to 0.109375
- span_order: int32 [32, 2], replicated, may hold values from 0 to 63, as said below
Outputs:
- attended: bfloat16 [16384, 6144], P(('ctx', 'tp'))
Inputs may be any that keep to these rules, and one draw needn't show every extreme that they name: `span_order`: row r is (p, 63 - p) with p a permutation of 0 to 31, so every span appears once.
All inputs are finite; a program needn't handle non-finite values.
Results may differ from a plain program's by a relative error of at most 0.014.
The roundings to bfloat16 on the way count: a program that leaves them out, or rounds other values in their place, can miss the bound.
Values may be sent and summed in bfloat16 or wider, within the bound.
No kernel may reach another device: no remote copies, remote signals or barrier semaphores. Data moves between devices by JAX's collectives and lax.ppermute only.
A program may use at most 128 MiB of HBM per device.

v0:
```python
import math
import jax
import jax.numpy as jnp
from jax import lax
from jax.sharding import PartitionSpec as P

ROPE_BASE = 1000000.0


def rotary_embed(values, token_positions):
    half = values.shape[-1] // 2
    freq = ROPE_BASE ** (-(jnp.arange(half, dtype=jnp.float32) * 2.0) / values.shape[-1])
    angle = token_positions[:, None] * freq[None, :]
    cosine = jnp.cos(angle)[:, None, :]
    sine = jnp.sin(angle)[:, None, :]
    first = values[..., :half]
    second = values[..., half:]
    return jnp.concatenate(
        [first * cosine - second * sine, second * cosine + first * sine], axis=-1
    )


def body(tokens, w_query, key_matrix, value_matrix, w_out, span_order):
    rank = lax.axis_index("ctx")
    head_dim = key_matrix.shape[1]
    qcols = w_query.shape[1]
    group = qcols // head_dim
    inv_scale = 1.0 / math.sqrt(head_dim)
    piece = lax.all_gather(tokens, "tp", axis=0, tiled=True)
    projected = jnp.concatenate(
        [
            jnp.dot(piece, w_query, preferred_element_type=jnp.float32),
            jnp.dot(piece, key_matrix, preferred_element_type=jnp.float32),
            jnp.dot(piece, value_matrix, preferred_element_type=jnp.float32),
        ],
        axis=1,
    )
    block_rows = projected.shape[0]
    span = block_rows // 2
    flat = span_order.reshape(-1)
    mine = lax.dynamic_slice(span_order, (rank, jnp.int32(0)), (1, 2)).reshape(2)
    own_pos = (
        (mine[:, None] * span + jnp.arange(span, dtype=jnp.int32)[None, :])
        .reshape(-1)
        .astype(jnp.float32)
    )
    query_rows = rotary_embed(
        projected[:, :qcols].reshape(block_rows, group, head_dim), own_pos
    ).astype(jnp.bfloat16)
    key = (
        rotary_embed(
            projected[:, qcols : qcols + head_dim].reshape(block_rows, 1, head_dim), own_pos
        )
        .reshape(block_rows, head_dim)
        .astype(jnp.bfloat16)
    )
    value_rows = projected[:, qcols + head_dim :].astype(jnp.bfloat16)
    query_rows = (
        query_rows.reshape(2, span, group, head_dim)
        .transpose(0, 2, 1, 3)
        .reshape(2, group * span, head_dim)
    )
    query_pos = jnp.tile(own_pos.reshape(2, 1, span), (1, group, 1)).reshape(2, group * span)

    def update(state, query_c, pos_c, key_tile, value_tile, key_pos):
        top_old, total_old, accum_old = state
        score = (
            lax.dot_general(
                query_c, key_tile, (((1,), (1,)), ((), ())), preferred_element_type=jnp.float32
            )
            * inv_scale
        )
        keep = key_pos[None, :] <= pos_c[:, None]
        score = jnp.where(keep, score, -1e30)
        top_new = jnp.maximum(top_old, jnp.max(score, axis=1))
        weight = jnp.where(keep, jnp.exp(score - top_new[:, None]), 0.0)
        factor = jnp.exp(top_old - top_new)
        total_new = factor * total_old + jnp.sum(weight, axis=1)
        accum_new = factor[:, None] * accum_old + jnp.dot(
            weight.astype(jnp.bfloat16), value_tile, preferred_element_type=jnp.float32
        )
        return (top_new, total_new, accum_new)

    rows_q = group * span
    start_top = jnp.full((rows_q,), -1e30, jnp.float32)
    start_total = jnp.zeros((rows_q,), jnp.float32)
    start_accum = jnp.zeros((rows_q, head_dim), jnp.float32)
    initial = (start_top, start_total, start_accum, start_top, start_total, start_accum)
    key_piece = lax.all_gather(key, "ctx", axis=0, tiled=True)
    value_piece = lax.all_gather(value_rows, "ctx", axis=0, tiled=True)
    count = key_piece.shape[0]
    global_rows = jnp.arange(count, dtype=jnp.int32)
    which = (global_rows // span)[:, None] == jnp.arange(flat.shape[0], dtype=jnp.int32)[None, :]
    span_ids = jnp.sum(jnp.where(which, flat[None, :], 0), axis=1)
    key_positions = (span_ids * span + global_rows % span).astype(jnp.float32)
    tile = math.gcd(count, span)

    def one_tile(step, state):
        key_tile = lax.dynamic_slice_in_dim(key_piece, step * tile, tile, 0)
        value_tile = lax.dynamic_slice_in_dim(value_piece, step * tile, tile, 0)
        pos_tile = lax.dynamic_slice_in_dim(key_positions, step * tile, tile, 0)
        updated = []
        for half_index in range(2):
            part_state = state[3 * half_index : 3 * half_index + 3]
            query_c = query_rows[half_index]
            pos_c = query_pos[half_index]
            needed = jnp.min(pos_tile) <= jnp.max(pos_c)
            part_state = lax.cond(
                needed,
                lambda inner: update(inner, query_c, pos_c, key_tile, value_tile, pos_tile),
                lambda inner: inner,
                part_state,
            )
            updated.extend(part_state)
        return tuple(updated)

    folded = lax.fori_loop(0, count // tile, one_tile, initial)
    halves = []
    for half_index in range(2):
        total = folded[3 * half_index + 1]
        accum = folded[3 * half_index + 2]
        mixed = (accum / total[:, None]).astype(jnp.bfloat16)
        halves.append(
            mixed.reshape(group, span, head_dim).transpose(1, 0, 2).reshape(span, group * head_dim)
        )
    heads_out = jnp.concatenate(halves, axis=0)
    return lax.psum_scatter(
        jnp.dot(heads_out, w_out, preferred_element_type=jnp.float32).astype(jnp.bfloat16),
        "tp",
        scatter_dimension=0,
        tiled=True,
    )


def solution(mesh):
    return jax.shard_map(
        body,
        mesh=mesh,
        in_specs=(
            P(("ctx", "tp"), None),
            P(None, "tp"),
            P(None, "tp"),
            P(None, "tp"),
            P("tp", None),
            P(),
        ),
        out_specs=P(("ctx", "tp"), None),
        check_vma=False,
    )
```

profile of v0, /device:TPU:1, one launch (start us, length us, event | category | flops | bytes accessed | tf_op | source)
XLA Modules:
  0.0 878.5 jit_solution(16667063462873135736)
XLA Ops:
  7.3 69.3 %all-gather.5.cloned.1.call-done = bf16[512,6144]{1,0:T(8,128)(2,1)} async-done(((bf16[128,6144]{1,0:T(8,128)(2,1)}), bf16[512,6144]{1,0:T(8,128)(2,1)}) %all-gather.5.cloned.1.call-update) | async-done | bytes 6291472 | tf_op jit(solution)/shard_map/all_gather | solution.py:29
  76.6 5.2 convolution_convert_fusion.1
  82.2 5.4 convolution_bitcast_fusion
  91.7 9.7 %fusion.50 = f32[512,768]{0,1:T(8,128)S(1)} fusion(bf16[512,6144]{1,0:T(8,128)(2,1)} %all-gather.5.cloned.1.call-done, bf16[6144,768]{1,0:T(8,128)(2,1)} %param.13), kind=kOutput, calls=%fused_computation.86 | convolution fusion | flops 4831838208 | bytes 17301504 | tf_op jit(solution)/shard_map/dot_general | solution.py:32
  104.6 57.0 %all-gather.7.cloned.1.call-done = bf16[16384,128]{1,0:T(8,128)(2,1)} async-done(((bf16[512,128]{1,0:T(8,128)(2,1)}), bf16[16384,128]{1,0:T(8,128)(2,1)}) %all-gather.7.cloned.1.call-update) | async-done | bytes 4194320 | tf_op jit(solution)/shard_map/all_gather | solution.py:90
  161.7 85.1 %all-gather.9.cloned.1.call-done = bf16[16384,1,128]{0,2,1:T(8,128)(2,1)} async-done(((bf16[512,1,128]{0,2,1:T(8,128)(2,1)}), bf16[16384,1,128]{0,2,1:T(8,128)(2,1)}) %all-gather.9.cloned.1.call-update) | async-done | bytes 4194320 | tf_op jit(solution)/shard_map/all_gather | solution.py:89
  246.9 550.0 %while.25 = (s32[]{:T(128)}, f32[1536]{0:T(1024)S(1)}, f32[1536]{0:T(1024)S(1)}, f32[1536,128]{1,0:T(8,128)S(1)}, f32[1536]{0:T(1024)S(1)}, /*index=5*/f32[1536]...) while((s32[]{:T(128)}, f32[1536]{0:T(1024)S(1)}, ...), condition=%wide.region_13.14_spmd.clone, body=%wide.region_3.13_spmd.clone.sunk | while | flops 412883200 | bytes 14330351 | solution.py:117
  255.4 2.6 conditional.7
  264.0 2.6 conditional.7
  275.1 2.6 conditional.7
  292.2 2.6 conditional.7
  309.3 2.6 conditional.7
  326.4 2.6 conditional.7
  343.5 2.6 conditional.7
  360.6 2.6 conditional.7
  377.8 2.6 conditional.7
  394.9 2.6 conditional.7
  412.0 2.6 conditional.7
  429.1 2.6 conditional.7
  446.2 2.6 conditional.7
  463.3 2.6 conditional.7
  480.4 2.6 conditional.7
  497.5 2.6 conditional.7
  514.6 2.6 conditional.7
  531.7 2.6 conditional.7
  548.8 2.6 conditional.7
  565.9 2.6 conditional.7
  583.0 2.6 conditional.7
  600.1 2.6 conditional.7
  617.2 2.6 conditional.7
  634.3 2.6 conditional.7
  651.4 2.6 conditional.7
  665.9 2.6 conditional.7
  674.5 2.6 conditional.7
  683.0 2.6 conditional.7
  691.6 2.6 conditional.7
  700.1 2.6 conditional.6
  702.7 2.6 conditional.7
  719.8 2.6 conditional.7
  734.3 2.6 conditional.6
  736.9 2.6 conditional.7
  751.4 2.6 conditional.7
  760.0 2.6 conditional.7
  768.5 2.6 conditional.6
  771.2 2.6 conditional.7
  788.3 2.6 conditional.7
  797.8 10.8 %convolution_convert_fusion = bf16[512,6144]{1,0:T(8,128)(2,1)} fusion(bf16[768,6144]{1,0:T(8,128)(2,1)} %param.16, bf16[256,768]{0,1:T(8,128)(2,1)S(1)} %bitcast.60, bf16[256,768]{0,1:T(8,128)(2,1)S(1)} %bitcast.61), kind=kOutput, calls=%fused_computation.36 | convolution fusion | flops 4836556800 | bytes 16515072 | tf_op jit(solution)/shard_map/dot_general | solution.py:128
  808.7 63.3 %reduce-scatter.2.cloned.1.call-done = bf16[128,6144]{1,0:T(8,128)(2,1)} async-done(((bf16[512,6144]{1,0:T(8,128)(2,1)}), bf16[128,6144]{1,0:T(8,128)(2,1)}) %reduce-scatter.2.cloned.1.call-update) | async-done | bytes 1572880 | tf_op jit(solution)/shard_map/reduce_scatter | solution.py:127
  (973 shorter events, 453.5 us)
Async XLA Ops:
  6.5 70.0 %copy-start = (bf16[6144,128]{1,0:T(8,128)(2,1)S(1)}, bf16[6144,128]{1,0:T(8,128)(2,1)}, u32[]{:S(2)}) copy-start(bf16[6144,128]{1,0:T(8,128)(2,1)} %param.15) | copy-start | bytes 4718596
  6.5 70.0 %all-gather.5.cloned.1.call-start = ((), (), s32[]{:S(2)}) async-start(), calls=%async_computation.1 | async-start | bytes 7864320 | tf_op jit(solution)/shard_map/all_gather | solution.py:29
  7.3 74.6 %copy-start.3 = (s32[32,2]{0,1:T(2,128)S(1)}, s32[32,2]{0,1:T(2,128)}, u32[]{:S(2)}) copy-start(s32[32,2]{0,1:T(2,128)} %param.17) | copy-start | bytes 772
  7.3 154.4 %all-gather.7.cloned.1.call-start = ((), (), s32[]{:S(2)}) async-start(), calls=%async_computation.2 | async-start | bytes 4325376 | tf_op jit(solution)/shard_map/all_gather | solution.py:90
  81.8 164.9 %all-gather.9.cloned.1.call-start = ((), (), s32[]{:S(2)}) async-start(), calls=%async_computation.4 | async-start | bytes 4325376 | tf_op jit(solution)/shard_map/all_gather | solution.py:89
  82.1 6.9 copy-start.1
  88.8 783.1 %reduce-scatter.2.cloned.1.call-start = ((), (), s32[]{:S(2)}) async-start(), calls=%async_computation.3 | async-start | bytes 7864320 | tf_op jit(solution)/shard_map/reduce_scatter | solution.py:127
  102.9 144.0 %copy-start.2 = (f32[2,256]{1,0:T(2,128)S(1)}, f32[2,256]{1,0:T(2,128)}, u32[]{:S(2)}) copy-start(f32[2,256]{1,0:T(2,128)} %copy-done.1) | copy-start | bytes 6148
Sparse Core Ops, SparseCore 0:
  9.0 67.5 all-gather.4
  81.9 79.6 all-gather.6
  164.4 82.2 all-gather.8
  808.8 63.1 reduce-scatter.1
where the time goes:
time: 892 us; the launch traced here: 878 us
  waiting for transfers between devices  275 us (31%)
  loops' own time  176 us (20%)
  matrix products  173 us (19%)
  local copies, waits for them, and re-layouts  121 us (14%)
  other arithmetic  120 us (13%)
  between operations  13.3 us (1%)
    another operation x1, loops' own time, body(): folded = lax.fori_loop(0, count // tile, one_tile, initial)  170 us
    reduce_min x64, other arithmetic, one_tile(): needed = jnp.min(pos_tile) <= jnp.max(pos_c)  91 us
    dot_general x65, matrix products, update(): lax.dot_general(query_c, key_tile, (((1,), (1,)), ((), ())), preferred_el...  89.9 us
    all_gather x1, waiting for transfers between devices, body(): key_piece = lax.all_gather(key, 'ctx', axis=0, tiled=True)  85.1 us
    all_gather x1, waiting for transfers between devices, body(): piece = lax.all_gather(tokens, 'tp', axis=0, tiled=True)  69.3 us
    reduce_scatter x1, waiting for transfers between devices, body(): lax.psum_scatter(jnp.dot(heads_out, w_out, preferred_element_type=jnp.flo...  63.3 us
    dynamic_slice x128, local copies, waits for them, and re-layouts, one_tile(): key_tile = lax.dynamic_slice_in_dim(key_piece, step * tile, tile, 0)  61.1 us
    all_gather x1, waiting for transfers between devices, body(): value_piece = lax.all_gather(value_rows, 'ctx', axis=0, tiled=True)  57 us
  transfers between devices with their start and end apart: 4, of which 4 were waited for; matrix products, arithmetic and copies ran while one was open for 3% of the time, Pallas kernels for 0%

commit v1 on v0

--- a/solution.py
+++ b/solution.py
@@ -86,7 +86,17 @@
     start_total = jnp.zeros((rows_q,), jnp.float32)
     start_accum = jnp.zeros((rows_q, head_dim), jnp.float32)
     initial = (start_top, start_total, start_accum, start_top, start_total, start_accum)
-    key_piece = lax.all_gather(key, "ctx", axis=0, tiled=True)
+
+    def lay_works_on(where_dim, vec, axis_tag):
+        f_next = jnp.concatenate(
+            lax.all_to_all(
+                jnp.stack([vec for _ in range(lax.axis_size(axis_tag))], 0), axis_tag, 0, 0
+            ),
+            where_dim,
+        )
+        return f_next
+
+    key_piece = lay_works_on(0, key, "ctx")
     value_piece = lax.all_gather(value_rows, "ctx", axis=0, tiled=True)
     count = key_piece.shape[0]
     global_rows = jnp.arange(count, dtype=jnp.int32)

time: 892 us -> 781 us (0.88)
  waiting for transfers between devices: 275 us -> 217 us
  local copies, waits for them, and re-layouts: 121 us -> 65 us
  starting transfers between devices: 0.12 us -> 9.32 us
    all_gather x1 -> x0, waiting for transfers between devices: 85.1 us -> none  [body(): key_piece = lax.all_gather(key, 'ctx', axis=0, tiled=True)]
    dynamic_slice x128 -> x0, local copies, waits for them, and re-layouts: 61.1 us -> none  [one_tile(): key_tile = lax.dynamic_slice_in_dim(key_piece, step * tile, tile, 0)]
    all_to_all x0 -> x1, waiting for transfers between devices: none -> 48.2 us  [lay_works_on(): lax.all_to_all(jnp.stack([vec for _ in range(lax.axis_size(axis_tag))], 0...]
    all_gather x1, waiting for transfers between devices: 57 us -> 36.4 us  [body(): value_piece = lax.all_gather(value_rows, 'ctx', axis=0, tiled=True)]
    all_to_all x0 -> x1, starting transfers between devices: none -> 9.23 us  [lay_works_on(): lax.all_to_all(jnp.stack([vec for _ in range(lax.axis_size(axis_tag))], 0...]
where the time goes in v1:
time: 781 us; the launch traced here: 770 us
  waiting for transfers between devices  217 us (28%)
  matrix products  173 us (22%)
  loops' own time  173 us (22%)
  other arithmetic  120 us (15%)
  local copies, waits for them, and re-layouts  65 us (8%)
  between operations  13.3 us (2%)
  starting transfers between devices  9.32 us (1%)
    another operation x1, loops' own time, body(): folded = lax.fori_loop(0, count // tile, one_tile, initial)  168 us
    reduce_min x64, other arithmetic, one_tile(): needed = jnp.min(pos_tile) <= jnp.max(pos_c)  91 us
    dot_general x65, matrix products, update(): lax.dot_general(query_c, key_tile, (((1,), (1,)), ((), ())), preferred_el...  89.9 us
    all_gather x1, waiting for transfers between devices, body(): piece = lax.all_gather(tokens, 'tp', axis=0, tiled=True)  69.3 us
    reduce_scatter x1, waiting for transfers between devices, body(): lax.psum_scatter(jnp.dot(heads_out, w_out, preferred_element_type=jnp.flo...  62.7 us
    dynamic_slice x64, local copies, waits for them, and re-layouts, one_tile(): value_tile = lax.dynamic_slice_in_dim(value_piece, step * tile, tile, 0)  56.9 us
    dot_general x65, matrix products, update(): jnp.dot(weight.astype(jnp.bfloat16), value_tile, preferred_element_type=j...  52.2 us
    all_to_all x1, waiting for transfers between devices, lay_works_on(): lax.all_to_all(jnp.stack([vec for _ in range(lax.axis_size(axis_tag))], 0...  48.2 us
  transfers between devices with their start and end apart: 4, of which 4 were waited for; matrix products, arithmetic and copies ran while one was open for 3% of the time, Pallas kernels for 0%

profile of v1, /device:TPU:1, one launch (start us, length us, event | category | flops | bytes accessed | tf_op | source)
XLA Modules:
  0.0 770.4 jit_solution(13357899131649554722)
XLA Ops:
  7.3 69.3 %all-gather.3.cloned.1.call-done = bf16[512,6144]{1,0:T(8,128)(2,1)} async-done(((bf16[128,6144]{1,0:T(8,128)(2,1)}), bf16[512,6144]{1,0:T(8,128)(2,1)}) %all-gather.3.cloned.1.call-update) | async-done | bytes 6291472 | tf_op jit(solution)/shard_map/all_gather | solution.py:29
  76.6 5.2 convolution_convert_fusion.1
  82.1 5.0 convolution_bitcast_fusion
  87.8 2.9 stack.2
  90.7 9.2 %all-to-all-start = ((bf16[32,512,128]{2,1,0:T(8,128)(2,1)}), bf16[32,512,128]{2,1,0:T(8,128)(2,1)}, u32[]{:S(2)}, u32[]{:S(2)}) async-start(bf16[32,512,128]{2,1,0:T(8,128)(2,1)} %stack.2), calls=%async_computation | async-start | bytes 8388608 | tf_op jit(solution)/shard_map/all_to_all | solution.py:92
  102.8 9.5 %fusion.50 = f32[512,768]{0,1:T(8,128)S(1)} fusion(bf16[512,6144]{1,0:T(8,128)(2,1)} %all-gather.3.cloned.1.call-done, bf16[6144,768]{1,0:T(8,128)(2,1)} %param.13), kind=kOutput, calls=%fused_computation.86 | convolution fusion | flops 4831838208 | bytes 17301504 | tf_op jit(solution)/shard_map/dot_general | solution.py:32
  115.7 48.2 %all-to-all-done = bf16[32,512,128]{2,1,0:T(8,128)(2,1)} async-done(((bf16[32,512,128]{2,1,0:T(8,128)(2,1)}), bf16[32,512,128]{2,1,0:T(8,128)(2,1)}, u32[]{:S(2)}, u32[]{:S(2)}) %all-to-all-start) | async-done | bytes 4194336 | tf_op jit(solution)/shard_map/all_to_all | solution.py:92
  163.9 36.4 %all-gather.5.cloned.1.call-done = bf16[16384,128]{1,0:T(8,128)(2,1)} async-done(((bf16[512,128]{1,0:T(8,128)(2,1)}), bf16[16384,128]{1,0:T(8,128)(2,1)}) %all-gather.5.cloned.1.call-update) | async-done | bytes 4194320 | tf_op jit(solution)/shard_map/all_gather | solution.py:100
  200.4 488.9 %while.25 = (s32[]{:T(128)}, f32[1536]{0:T(1024)S(1)}, f32[1536]{0:T(1024)S(1)}, f32[1536,128]{1,0:T(8,128)S(1)}, f32[1536]{0:T(1024)S(1)}, /*index=5*/f32[1536]...) while((s32[]{:T(128)}, f32[1536]{0:T(1024)S(1)}, ...), condition=%wide.region_13.14_spmd.clone, body=%wide.region_3.13_spmd.clone.sunk | while | flops 412883200 | bytes 14199275 | solution.py:127
  208.0 2.6 conditional.7
  215.6 2.6 conditional.7
  225.8 2.6 conditional.7
  241.0 2.6 conditional.7
  256.2 2.6 conditional.7
  271.4 2.6 conditional.7
  286.6 2.6 conditional.7
  301.7 2.6 conditional.7
  316.9 2.6 conditional.7
  332.1 2.6 conditional.7
  344.7 2.6 conditional.6
  347.3 2.6 conditional.7
  362.5 2.6 conditional.7
  377.7 2.6 conditional.7
  392.9 2.6 conditional.7
  408.1 2.6 conditional.7
  420.7 2.6 conditional.6
  423.3 2.6 conditional.7
  438.5 2.6 conditional.7
  453.7 2.6 conditional.7
  468.9 2.6 conditional.7
  484.1 2.6 conditional.7
  499.3 2.6 conditional.7
  514.5 2.6 conditional.7
  529.7 2.6 conditional.7
  544.9 2.6 conditional.7
  557.4 2.6 conditional.6
  560.1 2.6 conditional.7
  572.7 2.6 conditional.7
  580.3 2.6 conditional.7
  587.9 2.6 conditional.7
  595.5 2.6 conditional.7
  605.7 2.6 conditional.7
  620.9 2.6 conditional.7
  636.1 2.6 conditional.7
  648.7 2.6 conditional.7
  681.7 2.6 conditional.7
  690.3 10.8 %convolution_convert_fusion = bf16[512,6144]{1,0:T(8,128)(2,1)} fusion(bf16[768,6144]{1,0:T(8,128)(2,1)} %param.16, bf16[256,768]{0,1:T(8,128)(2,1)S(1)} %bitcast.62, bf16[256,768]{0,1:T(8,128)(2,1)S(1)} %bitcast.63), kind=kOutput, calls=%fused_computation.36 | convolution fusion | flops 4836556800 | bytes 16515072 | tf_op jit(solution)/shard_map/dot_general | solution.py:138
  701.1 62.7 %reduce-scatter.2.cloned.1.call-done = bf16[128,6144]{1,0:T(8,128)(2,1)} async-done(((bf16[512,6144]{1,0:T(8,128)(2,1)}), bf16[128,6144]{1,0:T(8,128)(2,1)}) %reduce-scatter.2.cloned.1.call-update) | async-done | bytes 1572880 | tf_op jit(solution)/shard_map/reduce_scatter | solution.py:137
  (848 shorter events, 399.6 us)
Async XLA Ops:
  6.5 70.0 %copy-start = (bf16[6144,128]{1,0:T(8,128)(2,1)S(1)}, bf16[6144,128]{1,0:T(8,128)(2,1)}, u32[]{:S(2)}) copy-start(bf16[6144,128]{1,0:T(8,128)(2,1)} %param.15) | copy-start | bytes 4718596
  6.5 70.0 %all-gather.3.cloned.1.call-start = ((), (), s32[]{:S(2)}) async-start(), calls=%async_computation.2 | async-start | bytes 7864320 | tf_op jit(solution)/shard_map/all_gather | solution.py:29
  7.3 74.6 %copy-start.4 = (s32[32,2]{0,1:T(2,128)S(1)}, s32[32,2]{0,1:T(2,128)}, u32[]{:S(2)}) copy-start(s32[32,2]{0,1:T(2,128)} %param.17) | copy-start | bytes 772
  7.3 74.8 %copy-start.1 = (bf16[6144,128]{1,0:T(8,128)(2,1)S(1)}, bf16[6144,128]{1,0:T(8,128)(2,1)}, u32[]{:S(2)}) copy-start(bf16[6144,128]{1,0:T(8,128)(2,1)} %param.14) | copy-start | bytes 4718596
  7.3 193.0 %all-gather.5.cloned.1.call-start = ((), (), s32[]{:S(2)}) async-start(), calls=%async_computation.3 | async-start | bytes 4325376 | tf_op jit(solution)/shard_map/all_gather | solution.py:100
  82.1 18.1 %copy-start.2 = (f32[2,256]{1,0:T(2,128)}, f32[2,256]{1,0:T(2,128)S(1)}, u32[]{:S(2)}) copy-start(f32[2,256]{1,0:T(2,128)S(1)} %get-tuple-element.576) | copy-start | bytes 6148
  90.7 73.1 %all-to-all-start = ((bf16[32,512,128]{2,1,0:T(8,128)(2,1)}), bf16[32,512,128]{2,1,0:T(8,128)(2,1)}, u32[]{:S(2)}, u32[]{:S(2)}) async-start(bf16[32,512,128]{2,1,0:T(8,128)(2,1)} %stack.2), calls=%async_computation | async-start | bytes 8388608 | tf_op jit(solution)/shard_map/all_to_all | solution.py:92
  100.0 663.9 %reduce-scatter.2.cloned.1.call-start = ((), (), s32[]{:S(2)}) async-start(), calls=%async_computation.4 | async-start | bytes 7864320 | tf_op jit(solution)/shard_map/reduce_scatter | solution.py:137
  113.9 86.5 %copy-start.3 = (f32[2,256]{1,0:T(2,128)S(1)}, f32[2,256]{1,0:T(2,128)}, u32[]{:S(2)}) copy-start(f32[2,256]{1,0:T(2,128)} %copy-done.2) | copy-start | bytes 6148
Sparse Core Ops, SparseCore 0:
  9.0 67.5 all-gather.2
  81.9 118.2 all-gather.4
  701.2 62.5 reduce-scatter.1
